TPU v7x, 32 devices: a whole 2x2x4 slice. The times are simulated.
32 devices in a mesh: row: 4 (over x, core), col: 8 (over z, y).
Axes of the slice: x: 2, y: 2, z: 4, core: 2. Of those that a mesh axis runs over, the one named last changes fastest.
Arguments:
- gate_act: bfloat16 [256, 14336], P(('row', 'col')), may hold values from -6 to 6
- up_act: bfloat16 [256, 14336], P(('row', 'col')), may hold values from -6 to 6
- running_hessian: float32 [14336, 14336], P('row', 'col'), may hold values from -0.03 to 2.02, as said below
Outputs:
- new_hessian: float32 [14336, 14336], P('row', 'col')
Inputs may be any that keep to these rules, and one draw needn't show every extreme that they name: `running_hessian`: symmetric.
All inputs are finite; a program needn't handle non-finite values.
Results may differ from a plain program's by a relative error of at most 0.0026.
Values may be sent and summed in bfloat16 or wider, within the bound.
A program may use at most 128 MiB of HBM per device.

v0:
```python
import jax
import jax.numpy as jnp
from jax import lax
from jax.sharding import PartitionSpec as P


def on_device(gate_act, up_act, running_hessian):
    n_row = lax.axis_size("row")
    n_col = lax.axis_size("col")
    tok_dev = gate_act.shape[0]
    col_width = running_hessian.shape[1]
    inputs = (jax.nn.silu(gate_act.astype(jnp.float32)) * up_act.astype(jnp.float32)).astype(
        jnp.bfloat16
    )
    col_part = lax.all_to_all(inputs, "col", split_axis=1, concat_axis=0, tiled=True)
    col_panel = lax.all_gather(col_part, "row", axis=0, tiled=True)
    col_ordered = (
        col_panel.reshape(n_row, n_col, tok_dev, col_width).swapaxes(0, 1).reshape(-1, col_width)
    )
    row_part = lax.all_to_all(inputs, "row", split_axis=1, concat_axis=0, tiled=True)
    gram = lax.dot_general(
        lax.all_gather(row_part, "col", axis=0, tiled=True),
        col_ordered,
        (((0,), (0,)), ((), ())),
        preferred_element_type=jnp.float32,
    )
    tokens_all = tok_dev * n_row * n_col
    total = 4.0 * tokens_all
    return 3.0 * tokens_all / total * running_hessian + 2.0 / total * gram


def solution(mesh):
    placed = (P(("row", "col"), None), P(("row", "col"), None), P("row", "col"))
    return jax.shard_map(
        on_device, mesh=mesh, in_specs=placed, out_specs=P("row", "col"), check_vma=False
    )
```

profile of v0, /device:TPU:0, one launch (start us, length us, event | category | flops | bytes accessed | tf_op | source)
XLA Modules:
  0.0 88.8 jit_solution(16086682137771318096)
XLA Ops:
  6.5 0.0 all-gather.2.cloned.1.call-start
  6.5 1.2 %fusion.4 = bf16[8,14336]{1,0:T(8,128)(2,1)S(1)} fusion(bf16[8,14336]{1,0:T(8,128)(2,1)} %param.4, bf16[8,14336]{1,0:T(8,128)(2,1)} %param.3), kind=kLoop, calls=%fused_computation.7 | loop fusion | flops 917504 | bytes 688128 | tf_op jit(solution)/shard_map/convert_element_type | solution.py:12
  7.7 9.8 %all_to_all.38 = bf16[8,4,3584]{2,0,1:T(8,128)(2,1)} all-to-all(bf16[8,4,3584]{2,0,1:T(8,128)(2,1)S(1)} %bitcast.16), channel_id=1, replica_groups=mesh['row'=4,'col'=8] {'row'}, dimensions={1} | all-to-all | bytes 458752 | tf_op jit(solution)/shard_map/all_to_all | solution.py:20
  17.5 0.0 all-gather.2.cloned.1.call-update
  17.5 16.4 %all_to_all.39 = bf16[8,8,1792]{2,0,1:T(8,128)(2,1)S(1)} all-to-all(bf16[8,8,1792]{2,0,1:T(8,128)(2,1)S(1)} %bitcast.17), channel_id=1, replica_groups=mesh['row'=4,'col'=8] {'col'}, dimensions={1} | all-to-all | bytes 458752 | tf_op jit(solution)/shard_map/all_to_all | solution.py:15
  33.9 7.6 %all_gather.7 = bf16[256,1792]{1,0:T(8,128)(2,1)S(1)} all-gather(bf16[64,1792]{1,0:T(8,128)(2,1)S(1)} %bitcast.19), channel_id=1, replica_groups=mesh['row'=4,'col'=8] {'row'}, dimensions={0}, use_global_device_ids=true | all-gather | bytes 1146880 | tf_op jit(solution)/shard_map/all_gather | solution.py:16
  41.5 0.1 copy.4
  41.6 23.6 %all-gather.2.cloned.1.call-done = bf16[256,3584]{1,0:T(8,128)(2,1)} async-done(((bf16[32,3584]{1,0:T(8,128)(2,1)}), bf16[256,3584]{1,0:T(8,128)(2,1)}) %all-gather.2.cloned.1.call-update) | async-done | bytes 1835024 | tf_op jit(solution)/shard_map/all_gather | solution.py:22
  65.2 16.8 %multiply_add_fusion = f32[3584,1792]{1,0:T(8,128)} fusion(f32[3584,1792]{1,0:T(8,128)} %param.5, bf16[256,3584]{1,0:T(8,128)(2,1)} %all-gather.2.cloned.1.call-done, bf16[256,1792]{1,0:T(8,128)(2,1)S(1)} %bitcast.14), kind=kOutput, calls=%fused_computation | convolution fusion | flops 3307601920 | bytes 54132736 | tf_op jit(solution)/shard_map/dot_general | solution.py:21
Async XLA Ops:
  6.5 58.6 %all-gather.2.cloned.1.call-start = ((), (), s32[]{:S(2)}) async-start(), calls=%async_computation.2 | async-start | bytes 2064384 | tf_op jit(solution)/shard_map/all_gather | solution.py:22
Sparse Core Ops, SparseCore 0:
  17.7 47.4 all-gather.1
where the time goes:
time: 89 us; the launch traced here: 88.8 us
  blocking collectives  33.7 us (38%)
  waiting for transfers between devices  23.6 us (27%)
  matrix products  16.8 us (19%)
  between operations  13.4 us (15%)
  other arithmetic  1.19 us (1%)
    all_gather x1, waiting for transfers between devices, on_device(): lax.all_gather(row_part, 'col', axis=0, tiled=True)  23.6 us
    dot_general x1, matrix products, on_device(): lax.dot_general(lax.all_gather(row_part, 'col', axis=0, tiled=True), col_...  16.8 us
    all_to_all x1, blocking collectives, on_device(): lax.all_to_all(inputs, 'col', split_axis=1, concat_axis=0, tiled=True)  16.4 us
    all_to_all x1, blocking collectives, on_device(): lax.all_to_all(inputs, 'row', split_axis=1, concat_axis=0, tiled=True)  9.8 us
    all_gather x1, blocking collectives, on_device(): col_panel = lax.all_gather(col_part, 'row', axis=0, tiled=True)  7.57 us
  transfers between devices with their start and end apart: 1, of which 1 were waited for; matrix products, arithmetic and copies ran while one was open for 0% of the time, Pallas kernels for 0%

commit v1 on v0

--- a/solution.py
+++ b/solution.py
@@ -1,17 +1,30 @@
+import functools
+
 import jax
 import jax.numpy as jnp
 from jax import lax
+from jax.experimental import pallas as pl
+from jax.experimental.pallas import tpu as pltpu
 from jax.sharding import PartitionSpec as P
 
-
-def on_device(gate_act, up_act, running_hessian):
+MESH = pl.DeviceIdType.MESH
+LANES = 128
+HESS_PARTS = 8
+LAG = 2
+
+
+def plain_inputs(gate_act, up_act):
+    return (jax.nn.silu(gate_act.astype(jnp.float32)) * up_act.astype(jnp.float32)).astype(
+        jnp.bfloat16
+    )
+
+
+def on_device_plain(gate_act, up_act, running_hessian):
     n_row = lax.axis_size("row")
     n_col = lax.axis_size("col")
     tok_dev = gate_act.shape[0]
     col_width = running_hessian.shape[1]
-    inputs = (jax.nn.silu(gate_act.astype(jnp.float32)) * up_act.astype(jnp.float32)).astype(
-        jnp.bfloat16
-    )
+    inputs = plain_inputs(gate_act, up_act)
     col_part = lax.all_to_all(inputs, "col", split_axis=1, concat_axis=0, tiled=True)
     col_panel = lax.all_gather(col_part, "row", axis=0, tiled=True)
     col_ordered = (
@@ -29,6 +42,262 @@
     return 3.0 * tokens_all / total * running_hessian + 2.0 / total * gram
 
 
+def other_core(r):
+    return r + 1 - 2 * lax.rem(r, 2)
+
+
+def gather_kernel(
+    n_row, n_col, gate_ref, up_ref, hess_hbm, row_ref, col_ref, hess_ref, own,
+    hess_sem, own_sem, x_send, x_recv, ring_send, ring_recv, c_send, c_recv, c_local,
+):
+    tok, width = gate_ref.shape[0], row_ref.shape[1]
+    half_width = col_ref.shape[1]
+    r, c = lax.axis_index("row"), lax.axis_index("col")
+    sib = other_core(r)
+    far = lax.rem(r + 2, n_row)
+    far_sib = other_core(far)
+    peers = (sib, far, far_sib)
+
+    y = lax.rem(c, 2)
+    place = (1 - y) * lax.div(c, 2) + y * (n_col - 1 - lax.div(c, 2))
+
+    def at(p):
+        p = lax.rem(p + 2 * n_col, n_col)
+        back = lax.div(p, n_col // 2)
+        return (1 - back) * 2 * p + back * (2 * (n_col - 1 - p) + 1)
+
+    nexts = (at(place + 1), at(place - 1))
+
+    hess_rows = hess_ref.shape[0] // HESS_PARTS
+    hess_copies = []
+    for i in range(HESS_PARTS):
+        part = pl.ds(i * hess_rows, hess_rows)
+        hess_copies.append(
+            pltpu.make_async_copy(hess_hbm.at[part], hess_ref.at[part], hess_sem.at[i])
+        )
+
+    barrier = pltpu.get_barrier_semaphore()
+    for peer in peers:
+        pl.semaphore_signal(barrier, inc=1, device_id={"row": peer, "col": c}, device_id_type=MESH)
+    for peer in nexts:
+        pl.semaphore_signal(barrier, inc=1, device_id={"row": r, "col": peer}, device_id_type=MESH)
+
+    gate = gate_ref[...].astype(jnp.float32)
+    own[...] = (jax.nn.silu(gate) * up_ref[...].astype(jnp.float32)).astype(jnp.bfloat16)
+
+    pl.semaphore_wait(barrier, len(peers) + 2)
+
+    def columns(row):
+        return pl.ds(pl.multiple_of(row * width, LANES), width)
+
+    my_rows = pl.ds(pl.multiple_of((c * n_row + r) * tok, tok), tok)
+    own_copy = pltpu.make_async_copy(own.at[:, columns(r)], row_ref.at[my_rows], own_sem)
+    swaps = []
+    for i, peer in enumerate(peers):
+        swaps.append(
+            pltpu.make_async_remote_copy(
+                src_ref=own.at[:, columns(peer)],
+                dst_ref=row_ref.at[my_rows],
+                send_sem=x_send.at[i],
+                recv_sem=x_recv.at[i],
+                device_id={"row": peer, "col": c},
+                device_id_type=MESH,
+            )
+        )
+    swaps[0].start()
+    own_copy.start()
+    swaps[1].start()
+    swaps[2].start()
+    for copy in hess_copies:
+        copy.start()
+
+    pair = 2 * tok
+    pair_of = (lax.div(r, 2), 1 - lax.div(r, 2))
+
+    def rows(source, g):
+        return pl.ds(pl.multiple_of((source * n_row + 2 * pair_of[g]) * tok, pair), pair)
+
+    def ring(d, s, g):
+        piece = rows(at(place - (s - 1) if d == 0 else place + (s - 1)), g)
+        return pltpu.make_async_remote_copy(
+            src_ref=row_ref.at[piece],
+            dst_ref=row_ref.at[piece],
+            send_sem=ring_send.at[d, s - 1, g],
+            recv_sem=ring_recv.at[d, s - 1, g],
+            device_id={"row": r, "col": nexts[d]},
+            device_id_type=MESH,
+        )
+
+    source_row = lax.div(c, 2)
+    is_source = r == source_row
+    is_sib = sib == source_row
+    is_far = far == source_row
+    is_last = far_sib == source_row
+    panel = pl.ds(pl.multiple_of(y * half_width, LANES), half_width)
+
+    def pieces(k):
+        if k < 2:
+            return c, k
+        d, s, g = events[k - 2]
+        return at(place - s if d == 0 else place + s), g
+
+    def col_rows(k):
+        source, g = pieces(k)
+        x_source = lax.div(source_row, 2)
+        p = x_source if g == 0 else 1 - x_source
+        return pl.ds(pl.multiple_of((source * n_row + 2 * p) * tok, pair), pair)
+
+    def col_copy(k, lane, target, src):
+        return pltpu.make_async_remote_copy(
+            src_ref=src,
+            dst_ref=col_ref.at[col_rows(k)],
+            send_sem=c_send.at[lane, k],
+            recv_sem=c_recv.at[k],
+            device_id={"row": target, "col": c},
+            device_id_type=MESH,
+        )
+
+    def from_rows(k, lane, target):
+        return col_copy(k, lane, target, row_ref.at[col_rows(k), panel])
+
+    def forward(k):
+        return col_copy(k, 0, sib, col_ref.at[col_rows(k)])
+
+    def local(k):
+        return pltpu.make_async_copy(
+            row_ref.at[col_rows(k), panel], col_ref.at[col_rows(k)], c_local.at[k]
+        )
+
+    hops = n_col // 2
+    events = [(d, s, g) for s in range(1, hops) for g in range(2) for d in range(2)]
+    events += [(0, hops, 0), (1, hops, 1)]
+    n_pieces = len(events) + 2
+
+    def share(k):
+        @pl.when(is_source)
+        def _():
+            from_rows(k, 1, far).start()
+            from_rows(k, 0, sib).start()
+            local(k).start()
+
+    def pass_on(k):
+        @pl.when(is_far)
+        def _():
+            forward(k).wait_recv()
+            forward(k).start()
+
+    swaps[0].wait_recv()
+    own_copy.wait()
+    for d in range(2):
+        ring(d, 1, 0).start()
+    share(0)
+    swaps[1].wait_recv()
+    swaps[2].wait_recv()
+    for d in range(2):
+        ring(d, 1, 1).start()
+    share(1)
+
+    for j, (d, s, g) in enumerate(events):
+        ring(d, s, g).wait_recv()
+        if (d, s + 1, g) in events:
+            ring(d, s + 1, g).start()
+        share(j + 2)
+        if j + 2 >= LAG:
+            pass_on(j + 2 - LAG)
+    for k in range(n_pieces - LAG, n_pieces):
+        pass_on(k)
+
+    for copy in hess_copies:
+        copy.wait()
+    for copy in swaps:
+        copy.wait_send()
+    for event in events:
+        ring(*event).wait_send()
+
+    @pl.when(is_source)
+    def _():
+        for k in range(n_pieces):
+            from_rows(k, 1, far).wait_send()
+            from_rows(k, 0, sib).wait_send()
+            local(k).wait()
+
+    @pl.when(is_far)
+    def _():
+        for k in range(n_pieces):
+            forward(k).wait_send()
+
+    @pl.when(jnp.logical_or(is_sib, is_last))
+    def _():
+        for k in range(n_pieces):
+            forward(k).wait_recv()
+
+
+def gram_kernel(keep, gain, row_ref, col_ref, hess_ref, out_ref):
+    tile = out_ref.shape[0]
+    i = pl.program_id(0)
+    lhs = row_ref[:, pl.ds(pl.multiple_of(i * tile, LANES), tile)]
+    gram = lax.dot_general(
+        lhs, col_ref[...], (((0,), (0,)), ((), ())), preferred_element_type=jnp.float32
+    )
+    old = hess_ref[pl.ds(pl.multiple_of(i * tile, LANES), tile), :]
+    out_ref[...] = keep * old + gain * gram
+
+
+def on_device(gate_act, up_act, running_hessian):
+    n_row = lax.axis_size("row")
+    n_col = lax.axis_size("col")
+    tok_dev = gate_act.shape[0]
+    height, col_width = running_hessian.shape
+    if n_row != 4 or n_col != 2 * n_row or col_width % LANES or tok_dev % 8:
+        return on_device_plain(gate_act, up_act, running_hessian)
+    tokens_all = tok_dev * n_row * n_col
+    total = 4.0 * tokens_all
+    vmem = pl.BlockSpec(memory_space=pltpu.VMEM)
+    hops = n_col // 2
+    n_pieces = 2 * n_col
+    dma = pltpu.SemaphoreType.DMA
+    row_panel, col_panel, old = pl.pallas_call(
+        functools.partial(gather_kernel, n_row, n_col),
+        out_shape=(
+            jax.ShapeDtypeStruct((tokens_all, height), jnp.bfloat16),
+            jax.ShapeDtypeStruct((tokens_all, col_width), jnp.bfloat16),
+            jax.ShapeDtypeStruct((height, col_width), jnp.float32),
+        ),
+        in_specs=[vmem, vmem, pl.BlockSpec(memory_space=pl.ANY)],
+        out_specs=(vmem, vmem, vmem),
+        scratch_shapes=[
+            pltpu.VMEM(gate_act.shape, jnp.bfloat16),
+            dma((HESS_PARTS,)),
+            dma(()),
+            dma((n_row - 1,)),
+            dma((n_row - 1,)),
+            dma((2, hops, 2)),
+            dma((2, hops, 2)),
+            dma((2, n_pieces)),
+            dma((n_pieces,)),
+            dma((n_pieces,)),
+        ],
+        compiler_params=pltpu.CompilerParams(
+            collective_id=0, has_side_effects=True, vmem_limit_bytes=VMEM_A
+        ),
+        name="gather",
+    )(gate_act, up_act, running_hessian)
+    tile = 2 * LANES
+    return pl.pallas_call(
+        functools.partial(gram_kernel, 3.0 * tokens_all / total, 2.0 / total),
+        out_shape=jax.ShapeDtypeStruct((height, col_width), jnp.float32),
+        grid=(height // tile,),
+        in_specs=[vmem, vmem, vmem],
+        out_specs=pl.BlockSpec((tile, col_width), lambda i: (i, 0)),
+        compiler_params=pltpu.CompilerParams(vmem_limit_bytes=VMEM_B),
+        name="gram",
+    )(row_panel, col_panel, old)
+
+
+VMEM_A = 8 * 2**20
+VMEM_B = 16 * 2**20
+
+
 def solution(mesh):
     placed = (P(("row", "col"), None), P(("row", "col"), None), P("row", "col"))
     return jax.shard_map(

time: 89 us -> 45.7 us (0.51)
  the two profiles are of different devices: /device:TPU:0 before, /device:TPU:17 now
where the time goes in v1:
time: 45.7 us; the launch traced here: 45.6 us
  Pallas kernels  43.7 us (96%)
  local copies, waits for them, and re-layouts  1.88 us (4%)
    pallas_call x1, Pallas kernels, on_device(): pl.pallas_call(functools.partial(gather_kernel, n_row, n_col), out_shape=...  31.3 us
    pallas_call x1, Pallas kernels, on_device(): pl.pallas_call(functools.partial(gram_kernel, 3.0 * tokens_all / total, 2...  12.4 us
    unnamed x4, local copies, waits for them, and re-layouts  1.88 us

profile of v1, /device:TPU:17, one launch (start us, length us, event | category | flops | bytes accessed | tf_op | source)
XLA Modules:
  0.0 45.6 jit_solution(6443167194807177286)
XLA Ops:
  0.0 0.0 copy-start
  0.0 0.9 %copy-done = bf16[8,14336]{1,0:T(8,128)(2,1)S(1)} copy-done((bf16[8,14336]{1,0:T(8,128)(2,1)S(1)}, bf16[8,14336]{1,0:T(8,128)(2,1)}, u32[]{:S(2)}) %copy-start) | copy-done | bytes 229400
  0.9 0.0 copy-start.1
  0.9 0.9 %copy-done.1 = bf16[8,14336]{1,0:T(8,128)(2,1)S(1)} copy-done((bf16[8,14336]{1,0:T(8,128)(2,1)S(1)}, bf16[8,14336]{1,0:T(8,128)(2,1)}, u32[]{:S(2)}) %copy-start.1) | copy-done | bytes 229400
  1.9 31.3 %gather.1 = (bf16[256,3584]{1,0:T(8,128)(2,1)S(1)}, bf16[256,1792]{1,0:T(8,128)(2,1)S(1)}, f32[3584,1792]{1,0:T(8,128)S(1)}) custom-call(bf16[8,14336]{1,0:T(8,128)(2,1)S(1)} %copy-done, bf16[8,14336]{1,0:T(8,128)(2,1)S(1)} %copy-done.1, f32[3584,1792]{1,0:T(8,128)} %hess_hbm.1), custom_call_target="tpu_custom_call" | custom-call | tf_op jit(solution)/shard_map/gather/pallas_call | solution.py:259
  33.2 12.4 %gram.1 = f32[3584,1792]{1,0:T(8,128)} custom-call(bf16[256,3584]{1,0:T(8,128)(2,1)S(1)} %get-tuple-element.8.row_ref, bf16[256,1792]{1,0:T(8,128)(2,1)S(1)} %get-tuple-element.9.col_ref, f32[3584,1792]{1,0:T(8,128)S(1)} %get-tuple-element.10.hess_ref), custom_call_target="tpu_custom_call" | custom-call | tf_op jit(solution)/shard_map/gram/pallas_call | solution.py:286
Async XLA Ops:
  0.0 0.9 %copy-start = (bf16[8,14336]{1,0:T(8,128)(2,1)S(1)}, bf16[8,14336]{1,0:T(8,128)(2,1)}, u32[]{:S(2)}) copy-start(bf16[8,14336]{1,0:T(8,128)(2,1)} %gate_ref.1) | copy-start | bytes 688132
  0.9 0.9 %copy-start.1 = (bf16[8,14336]{1,0:T(8,128)(2,1)S(1)}, bf16[8,14336]{1,0:T(8,128)(2,1)}, u32[]{:S(2)}) copy-start(bf16[8,14336]{1,0:T(8,128)(2,1)} %up_ref.1) | copy-start | bytes 688132

commit v2 on v1

--- a/solution.py
+++ b/solution.py
@@ -47,9 +47,13 @@
 
 
 def gather_kernel(
-    n_row, n_col, gate_ref, up_ref, hess_hbm, row_ref, col_ref, hess_ref, own,
-    hess_sem, own_sem, x_send, x_recv, ring_send, ring_recv, c_send, c_recv, c_local,
+    n_row, n_col, gate_hbm, up_hbm, hess_hbm, row_ref, col_ref, hess_ref, gate_ref, up_ref, own,
+    in_sem, hess_sem, own_sem, x_send, x_recv, ring_send, ring_recv, c_send, c_recv, c_local,
 ):
+    gate_copy = pltpu.make_async_copy(gate_hbm, gate_ref, in_sem.at[0])
+    up_copy = pltpu.make_async_copy(up_hbm, up_ref, in_sem.at[1])
+    gate_copy.start()
+    up_copy.start()
     tok, width = gate_ref.shape[0], row_ref.shape[1]
     half_width = col_ref.shape[1]
     r, c = lax.axis_index("row"), lax.axis_index("col")
@@ -82,6 +86,8 @@
     for peer in nexts:
         pl.semaphore_signal(barrier, inc=1, device_id={"row": r, "col": peer}, device_id_type=MESH)
 
+    gate_copy.wait()
+    up_copy.wait()
     gate = gate_ref[...].astype(jnp.float32)
     own[...] = (jax.nn.silu(gate) * up_ref[...].astype(jnp.float32)).astype(jnp.bfloat16)
 
@@ -104,29 +110,41 @@
                 device_id_type=MESH,
             )
         )
-    swaps[0].start()
-    own_copy.start()
-    swaps[1].start()
-    swaps[2].start()
-    for copy in hess_copies:
-        copy.start()
-
     pair = 2 * tok
     pair_of = (lax.div(r, 2), 1 - lax.div(r, 2))
 
     def rows(source, g):
         return pl.ds(pl.multiple_of((source * n_row + 2 * pair_of[g]) * tok, pair), pair)
 
-    def ring(d, s, g):
-        piece = rows(at(place - (s - 1) if d == 0 else place + (s - 1)), g)
+    hops = n_col // 2
+
+    def to_next(d, s, g, src, dst):
         return pltpu.make_async_remote_copy(
-            src_ref=row_ref.at[piece],
-            dst_ref=row_ref.at[piece],
+            src_ref=src,
+            dst_ref=dst,
             send_sem=ring_send.at[d, s - 1, g],
             recv_sem=ring_recv.at[d, s - 1, g],
             device_id={"row": r, "col": nexts[d]},
             device_id_type=MESH,
         )
+
+    def ring(d, s, g):
+        piece = row_ref.at[rows(at(place - (s - 1) if d == 0 else place + (s - 1)), g)]
+        return to_next(d, s, g, piece, piece)
+
+    def last_hop(d, g, second):
+        y_next = lax.rem(nexts[d], 2)
+        side = 1 - y_next if second else y_next
+        piece = row_ref.at[
+            rows(at(place - (hops - 1) if d == 0 else place + (hops - 1)), g),
+            pl.ds(pl.multiple_of(side * half_width, LANES), half_width),
+        ]
+        return to_next(d, hops, 1 - g if second else g, piece, piece)
+
+    def start_first(g, source, src=None):
+        block = row_ref.at[pl.ds(pl.multiple_of((c * n_row + source) * tok, tok), tok)]
+        for d in range(2):
+            to_next(d, 1, g, block if src is None else src, block).start()
 
     source_row = lax.div(c, 2)
     is_source = r == source_row
@@ -168,15 +186,25 @@
             row_ref.at[col_rows(k), panel], col_ref.at[col_rows(k)], c_local.at[k]
         )
 
-    hops = n_col // 2
     events = [(d, s, g) for s in range(1, hops) for g in range(2) for d in range(2)]
-    events += [(0, hops, 0), (1, hops, 1)]
+    finals = [(0, hops, 0), (1, hops, 1)]
+    events += finals
     n_pieces = len(events) + 2
+
+    n_direct = len(finals)
+
+    def direct(k):
+        return k >= n_pieces - n_direct
+
+    def straight(k):
+        return from_rows(k, 2, far_sib)
 
     def share(k):
         @pl.when(is_source)
         def _():
             from_rows(k, 1, far).start()
+            if direct(k):
+                straight(k).start()
             from_rows(k, 0, sib).start()
             local(k).start()
 
@@ -184,22 +212,35 @@
         @pl.when(is_far)
         def _():
             forward(k).wait_recv()
-            forward(k).start()
-
+            if not direct(k):
+                forward(k).start()
+
+    start_first(0, r, own.at[:, columns(r)])
+    swaps[0].start()
+    swaps[1].start()
+    swaps[2].start()
+    own_copy.start()
+    for copy in hess_copies:
+        copy.start()
     swaps[0].wait_recv()
+    start_first(0, sib)
     own_copy.wait()
-    for d in range(2):
-        ring(d, 1, 0).start()
     share(0)
     swaps[1].wait_recv()
+    start_first(1, far)
     swaps[2].wait_recv()
-    for d in range(2):
-        ring(d, 1, 1).start()
+    start_first(1, far_sib)
     share(1)
 
     for j, (d, s, g) in enumerate(events):
-        ring(d, s, g).wait_recv()
-        if (d, s + 1, g) in events:
+        if s < hops:
+            ring(d, s, g).wait_recv()
+        else:
+            last_hop(d, g, False).wait_recv()
+        if (d, s + 1, g) in finals:
+            last_hop(d, g, False).start()
+            last_hop(d, g, True).start()
+        elif (d, s + 1, g) in events:
             ring(d, s + 1, g).start()
         share(j + 2)
         if j + 2 >= LAG:
@@ -211,8 +252,13 @@
         copy.wait()
     for copy in swaps:
         copy.wait_send()
-    for event in events:
-        ring(*event).wait_send()
+    for d, s, g in events:
+        if s < hops:
+            ring(d, s, g).wait_send()
+        else:
+            last_hop(d, g, True).wait_recv()
+            last_hop(d, g, False).wait_send()
+            last_hop(d, g, True).wait_send()
 
     @pl.when(is_source)
     def _():
@@ -220,11 +266,14 @@
             from_rows(k, 1, far).wait_send()
             from_rows(k, 0, sib).wait_send()
             local(k).wait()
+            if direct(k):
+                straight(k).wait_send()
 
     @pl.when(is_far)
     def _():
         for k in range(n_pieces):
-            forward(k).wait_send()
+            if not direct(k):
+                forward(k).wait_send()
 
     @pl.when(jnp.logical_or(is_sib, is_last))
     def _():
@@ -252,6 +301,7 @@
         return on_device_plain(gate_act, up_act, running_hessian)
     tokens_all = tok_dev * n_row * n_col
     total = 4.0 * tokens_all
+    in_hbm = functools.partial(pltpu.with_memory_space_constraint, memory_space=pltpu.HBM)
     vmem = pl.BlockSpec(memory_space=pltpu.VMEM)
     hops = n_col // 2
     n_pieces = 2 * n_col
@@ -263,17 +313,20 @@
             jax.ShapeDtypeStruct((tokens_all, col_width), jnp.bfloat16),
             jax.ShapeDtypeStruct((height, col_width), jnp.float32),
         ),
-        in_specs=[vmem, vmem, pl.BlockSpec(memory_space=pl.ANY)],
+        in_specs=[pl.BlockSpec(memory_space=pltpu.HBM)] * 3,
         out_specs=(vmem, vmem, vmem),
         scratch_shapes=[
             pltpu.VMEM(gate_act.shape, jnp.bfloat16),
+            pltpu.VMEM(gate_act.shape, jnp.bfloat16),
+            pltpu.VMEM(gate_act.shape, jnp.bfloat16),
+            dma((2,)),
             dma((HESS_PARTS,)),
             dma(()),
             dma((n_row - 1,)),
             dma((n_row - 1,)),
             dma((2, hops, 2)),
             dma((2, hops, 2)),
-            dma((2, n_pieces)),
+            dma((3, n_pieces)),
             dma((n_pieces,)),
             dma((n_pieces,)),
         ],
@@ -281,8 +334,8 @@
             collective_id=0, has_side_effects=True, vmem_limit_bytes=VMEM_A
         ),
         name="gather",
-    )(gate_act, up_act, running_hessian)
-    tile = 2 * LANES
+    )(in_hbm(gate_act), in_hbm(up_act), running_hessian)
+    tile = height // 7 if height % (7 * LANES) == 0 else LANES
     return pl.pallas_call(
         functools.partial(gram_kernel, 3.0 * tokens_all / total, 2.0 / total),
         out_shape=jax.ShapeDtypeStruct((height, col_width), jnp.float32),
@@ -295,7 +348,7 @@
 
 
 VMEM_A = 8 * 2**20
-VMEM_B = 16 * 2**20
+VMEM_B = 24 * 2**20
 
 
 def solution(mesh):

time: 45.7 us -> 39.1 us (0.86)
  the two profiles are of different devices: /device:TPU:17 before, /device:TPU:0 now
where the time goes in v2:
time: 39.1 us; the launch traced here: 39 us
  Pallas kernels  38.9 us (99%)
    pallas_call x1, Pallas kernels, on_device(): pl.pallas_call(functools.partial(gather_kernel, n_row, n_col), out_shape=...  28.8 us
    pallas_call x1, Pallas kernels, on_device(): pl.pallas_call(functools.partial(gram_kernel, 3.0 * tokens_all / total, 2...  10.1 us

profile of v2, /device:TPU:0, one launch (start us, length us, event | category | flops | bytes accessed | tf_op | source)
XLA Modules:
  0.0 39.0 jit_solution(13130930779911276364)
XLA Ops:
  0.0 28.8 %gather.1 = (bf16[256,3584]{1,0:T(8,128)(2,1)S(1)}, bf16[256,1792]{1,0:T(8,128)(2,1)S(1)}, f32[3584,1792]{1,0:T(8,128)S(1)}) custom-call(bf16[8,14336]{1,0:T(8,128)(2,1)} %gate_hbm.1, bf16[8,14336]{1,0:T(8,128)(2,1)} %up_hbm.1, f32[3584,1792]{1,0:T(8,128)} %hess_hbm.1), custom_call_target="tpu_custom_call" | custom-call | tf_op jit(solution)/shard_map/gather/pallas_call | solution.py:309
  28.8 10.1 %gram.1 = f32[3584,1792]{1,0:T(8,128)} custom-call(bf16[256,3584]{1,0:T(8,128)(2,1)S(1)} %get-tuple-element.8.row_ref, bf16[256,1792]{1,0:T(8,128)(2,1)S(1)} %get-tuple-element.9.col_ref, f32[3584,1792]{1,0:T(8,128)S(1)} %get-tuple-element.10.hess_ref), custom_call_target="tpu_custom_call" | custom-call | tf_op jit(solution)/shard_map/gram/pallas_call | solution.py:339

commit v3 on v2

--- a/solution.py
+++ b/solution.py
@@ -281,15 +281,50 @@
             forward(k).wait_recv()
 
 
-def gram_kernel(keep, gain, row_ref, col_ref, hess_ref, out_ref):
-    tile = out_ref.shape[0]
-    i = pl.program_id(0)
-    lhs = row_ref[:, pl.ds(pl.multiple_of(i * tile, LANES), tile)]
-    gram = lax.dot_general(
-        lhs, col_ref[...], (((0,), (0,)), ((), ())), preferred_element_type=jnp.float32
-    )
-    old = hess_ref[pl.ds(pl.multiple_of(i * tile, LANES), tile), :]
-    out_ref[...] = keep * old + gain * gram
+def gram_kernel(keep, gain, strips, row_ref, col_ref, hess_ref, out_hbm, tiles, sems):
+    tile = tiles.shape[1]
+    i, n = pl.program_id(0), pl.num_programs(0)
+    slot = lax.rem(i, 2)
+
+    def copies(at_slot, at_tile):
+        rows = pl.ds(pl.multiple_of(at_tile * tile, LANES), tile)
+        return [
+            pltpu.make_async_copy(
+                tiles.at[at_slot, :, pl.ds(start, size)],
+                out_hbm.at[rows, pl.ds(start, size)],
+                sems.at[at_slot, k],
+            )
+            for k, (start, size) in enumerate(strips)
+        ]
+
+    @pl.when(i >= 2)
+    def _():
+        for copy in copies(slot, i - 2):
+            copy.wait()
+
+    rows = pl.ds(pl.multiple_of(i * tile, LANES), tile)
+    out = copies(slot, i)
+    for k, (start, size) in enumerate(strips):
+        strip = slice(start, start + size)
+        gram = lax.dot_general(
+            row_ref[:, rows],
+            col_ref[:, strip],
+            (((0,), (0,)), ((), ())),
+            preferred_element_type=jnp.float32,
+        )
+        tiles[slot, :, strip] = keep * hess_ref[rows, strip] + gain * gram
+        out[k].start()
+
+    @pl.when(i == n - 1)
+    def _():
+        for copy in copies(1 - slot, i - 1) + out:
+            copy.wait()
+
+
+def column_strips(width, count):
+    blocks = width // LANES
+    edges = [LANES * (blocks * k // count) for k in range(count + 1)]
+    return [(a, b - a) for a, b in zip(edges, edges[1:])]
 
 
 def on_device(gate_act, up_act, running_hessian):
@@ -336,17 +371,20 @@
         name="gather",
     )(in_hbm(gate_act), in_hbm(up_act), running_hessian)
     tile = height // 7 if height % (7 * LANES) == 0 else LANES
+    strips = column_strips(col_width, STRIPS)
     return pl.pallas_call(
-        functools.partial(gram_kernel, 3.0 * tokens_all / total, 2.0 / total),
+        functools.partial(gram_kernel, 3.0 * tokens_all / total, 2.0 / total, strips),
         out_shape=jax.ShapeDtypeStruct((height, col_width), jnp.float32),
         grid=(height // tile,),
         in_specs=[vmem, vmem, vmem],
-        out_specs=pl.BlockSpec((tile, col_width), lambda i: (i, 0)),
+        out_specs=pl.BlockSpec(memory_space=pltpu.HBM),
+        scratch_shapes=[pltpu.VMEM((2, tile, col_width), jnp.float32), dma((2, len(strips)))],
         compiler_params=pltpu.CompilerParams(vmem_limit_bytes=VMEM_B),
         name="gram",
     )(row_panel, col_panel, old)
 
 
+STRIPS = 7
 VMEM_A = 8 * 2**20
 VMEM_B = 24 * 2**20
 

time: 39.1 us -> 37.9 us (0.969)
  Pallas kernels: 38.9 us -> 37.7 us
    pallas_call x1, Pallas kernels: 10.1 us -> 8.89 us  [on_device(): pl.pallas_call(functools.partial(gram_kernel, 3.0 * tokens_all / total, 2...]
where the time goes in v3:
time: 37.9 us; the launch traced here: 37.7 us
  Pallas kernels  37.7 us (99%)
    pallas_call x1, Pallas kernels, on_device(): pl.pallas_call(functools.partial(gather_kernel, n_row, n_col), out_shape=...  28.8 us
    pallas_call x1, Pallas kernels, on_device(): pl.pallas_call(functools.partial(gram_kernel, 3.0 * tokens_all / total, 2...  8.89 us

profile of v3, /device:TPU:0, one launch (start us, length us, event | category | flops | bytes accessed | tf_op | source)
XLA Modules:
  0.0 37.7 jit_solution(5506689612492032055)
XLA Ops:
  0.0 28.8 %gather.1 = (bf16[256,3584]{1,0:T(8,128)(2,1)S(1)}, bf16[256,1792]{1,0:T(8,128)(2,1)S(1)}, f32[3584,1792]{1,0:T(8,128)S(1)}) custom-call(bf16[8,14336]{1,0:T(8,128)(2,1)} %gate_hbm.1, bf16[8,14336]{1,0:T(8,128)(2,1)} %up_hbm.1, f32[3584,1792]{1,0:T(8,128)} %hess_hbm.1), custom_call_target="tpu_custom_call" | custom-call | tf_op jit(solution)/shard_map/gather/pallas_call | solution.py:344
  28.8 8.9 %gram.1 = f32[3584,1792]{1,0:T(8,128)} custom-call(bf16[256,3584]{1,0:T(8,128)(2,1)S(1)} %get-tuple-element.8.row_ref, bf16[256,1792]{1,0:T(8,128)(2,1)S(1)} %get-tuple-element.9.col_ref, f32[3584,1792]{1,0:T(8,128)S(1)} %get-tuple-element.10.hess_ref), custom_call_target="tpu_custom_call" | custom-call | tf_op jit(solution)/shard_map/gram/pallas_call | solution.py:375
